TPU v7x, 512 devices: a whole 4x8x8 slice. The times are simulated.
512 devices in a mesh: seq: 64 (over z, y), req: 8 (over x, core).
Axes of the slice: x: 4, y: 8, z: 8, core: 2. Of those that a mesh axis runs over, the one named last changes fastest.
Arguments:
- hidden_in: bfloat16 [128, 4, 2048], P('req'), may hold values from -6 to 6
- attn_gain: float32 [2048], replicated, may hold values from 0.5 to 1.5
- q_gain: float32 [256], replicated, may hold values from 0.5 to 1.5
- k_gain: float32 [256], replicated, may hold values from 0.5 to 1.5
- post_attn_gain: float32 [2048], replicated, may hold values from 0.5 to 1.5
- ffn_gain: float32 [2048], replicated, may hold values from 0.5 to 1.5
- post_ffn_gain: float32 [2048], replicated, may hold values from 0.5 to 1.5
- w_qkv: bfloat16 [2048, 3072], P('seq', 'req'), may hold values from -0.125 to 0.125
- w_out: bfloat16 [2048, 2048], P('seq', 'req'), may hold values from -0.125 to 0.125
- w_gate: bfloat16 [2048, 8192], P('req', 'seq'), may hold values from -0.125 to 0.125
- w_up: bfloat16 [2048, 8192], P('req', 'seq'), may hold values from -0.125 to 0.125
- w_down: bfloat16 [8192, 2048], P('seq', 'req'), may hold values from -0.0625 to 0.0625
- prompt_keys: bfloat16 [16, 8192, 512], P('req', 'seq')
- prompt_values: bfloat16 [16, 8192, 512], P('req', 'seq'), may hold values from -6 to 6
- tail_keys: bfloat16 [8, 16384, 512], P('req', 'seq')
- tail_values: bfloat16 [8, 16384, 512], P('req', 'seq'), may hold values from -6 to 6
- group_of: int32 [128], P('req'), may hold values from 0 to 15, as said below
- prompt_lengths: int32 [16], P('req'), may hold values from 1 to 8192
- tail_lengths: int32 [128], P('req'), may hold values from 1 to 1024
- page_table: int32 [8, 1024], P('req'), may hold values from 0 to 1023, each once within a row
Outputs:
- layer_out: bfloat16 [128, 4, 2048], P('req')
Inputs may be any that keep to these rules, and one draw needn't show every extreme that they name: `group_of`: request i belongs to one of the 2 groups i // 16 * 2 to i // 16 * 2 + 1 of its own block of requests. `page_table`: each row lists every pool page of its index of req once; entry j * 64 + p is the pool page of page p of the j-th request of that block.
All inputs are finite; a program needn't handle non-finite values.
Results may differ from a plain program's by a relative error of at most 0.012.
The roundings to bfloat16 on the way count: a program that leaves them out, or rounds other values in their place, can miss the bound.
Values may be sent and summed in bfloat16 or wider, within the bound.
A program may use at most 128 MiB of HBM per device.

v0:
```python
import jax
import jax.numpy as jnp
from jax import lax
from jax.sharding import PartitionSpec as P

D = 2048
H = 8
KV = 2
HD = 256
PAGE = 16
QKV = 3072
EPSILON = 1e-06
NEGATIVE = -1e30


def normalize(values):
    return values * lax.rsqrt(jnp.mean(values * values, axis=-1, keepdims=True) + EPSILON)


def on_device(
    hidden_in,
    attn_gain,
    q_gain,
    k_gain,
    post_attn_gain,
    ffn_gain,
    post_ffn_gain,
    w_qkv,
    w_out,
    w_gate,
    w_up,
    w_down,
    prompt_keys,
    prompt_values,
    tail_keys,
    tail_values,
    group_of,
    prompt_lengths,
    tail_lengths,
    page_table,
):
    seq_index = lax.axis_index("seq")
    rows_req = hidden_in.shape[0]
    step_count = hidden_in.shape[1]
    group_size = H // KV
    tokens = rows_req * step_count
    hidden = hidden_in.astype(jnp.float32)
    normed = (normalize(hidden) * attn_gain).astype(jnp.bfloat16)
    in_rows = w_qkv.shape[0]
    normed_cols = lax.dynamic_slice_in_dim(normed, seq_index * in_rows, in_rows, 2).reshape(
        tokens, in_rows
    )
    qkv_full, out_full, gate_full, up_full, down_full = (
        lax.all_gather(w_qkv, "req", axis=1, tiled=True),
        lax.all_gather(w_out, "req", axis=1, tiled=True),
        lax.all_gather(w_gate, "req", axis=0, tiled=True),
        lax.all_gather(w_up, "req", axis=0, tiled=True),
        lax.all_gather(w_down, "req", axis=1, tiled=True),
    )
    qkv_part = jnp.dot(normed_cols, qkv_full, preferred_element_type=jnp.float32)
    projected = lax.psum(qkv_part, "seq").reshape(rows_req, step_count, QKV)
    queries = (
        normalize(projected[..., : H * HD].reshape(rows_req, step_count, H, HD)) * q_gain
    ).astype(jnp.bfloat16)
    keys_new = (
        normalize(projected[..., H * HD : (H + KV) * HD].reshape(rows_req, step_count, KV, HD))
        * k_gain
    ).astype(jnp.bfloat16)
    values_new = normalize(
        projected[..., (H + KV) * HD :].reshape(rows_req, step_count, KV, HD)
    ).astype(jnp.bfloat16)
    query_groups = queries.reshape(rows_req, step_count, KV, group_size, HD)
    group_count = prompt_keys.shape[0]
    prompt_span = prompt_keys.shape[1]
    cache_keys = prompt_keys.reshape(group_count, prompt_span, KV, HD)
    cache_values = prompt_values.reshape(group_count, prompt_span, KV, HD)
    member = (group_of % group_count)[:, None] == jnp.arange(group_count, dtype=jnp.int32)[None, :]
    prompt_pos = seq_index * prompt_span + jnp.arange(prompt_span, dtype=jnp.int32)
    prompt_live = prompt_pos[None, :] < prompt_lengths[:, None]
    prompt_mask = (member[:, :, None] & prompt_live[None, :, :])[:, None, None, None, :, :]
    prompt_scores = jnp.einsum(
        "rskgd,cpkd->rskgcp", query_groups, cache_keys, preferred_element_type=jnp.float32
    )
    prompt_scores = jnp.where(prompt_mask, prompt_scores, NEGATIVE)
    pool_rows = tail_keys.shape[1]
    slot_count = pool_rows // PAGE
    table_row = page_table[0]
    table_len = table_row.shape[0]
    tail_pages = table_len // rows_req
    slot_ids = seq_index * slot_count + jnp.arange(slot_count, dtype=jnp.int32)
    matches = table_row[None, :] == slot_ids[:, None]
    entries = jnp.sum(
        jnp.where(matches, jnp.arange(table_len, dtype=jnp.int32)[None, :], 0), axis=1
    )
    owners = jnp.repeat(entries // tail_pages, PAGE)
    tail_pos = jnp.repeat(entries % tail_pages, PAGE) * PAGE + jnp.tile(
        jnp.arange(PAGE, dtype=jnp.int32), slot_count
    )
    tail_mask = (owners[None, :] == jnp.arange(rows_req, dtype=jnp.int32)[:, None]) & (
        tail_pos[None, :] < tail_lengths[:, None]
    )
    tail_mask = tail_mask[:, None, None, None, :]
    pool_keys = tail_keys[0].reshape(pool_rows, KV, HD)
    pool_values = tail_values[0].reshape(pool_rows, KV, HD)
    tail_scores = jnp.einsum(
        "rskgd,pkd->rskgp", query_groups, pool_keys, preferred_element_type=jnp.float32
    )
    tail_scores = jnp.where(tail_mask, tail_scores, NEGATIVE)
    block_top = jnp.maximum(jnp.max(prompt_scores, axis=(4, 5)), jnp.max(tail_scores, axis=4))
    prompt_probs = jnp.where(prompt_mask, jnp.exp(prompt_scores - block_top[..., None, None]), 0.0)
    tail_probs = jnp.where(tail_mask, jnp.exp(tail_scores - block_top[..., None]), 0.0)
    block_total = jnp.sum(prompt_probs, axis=(4, 5)) + jnp.sum(tail_probs, axis=4)
    block_accum = jnp.einsum(
        "rskgcp,cpkd->rskgd",
        prompt_probs.astype(jnp.bfloat16),
        cache_values,
        preferred_element_type=jnp.float32,
    )
    block_accum = block_accum + jnp.einsum(
        "rskgp,pkd->rskgd",
        tail_probs.astype(jnp.bfloat16),
        pool_values,
        preferred_element_type=jnp.float32,
    )
    new_scores = jnp.einsum(
        "rskgd,rukd->rskgu", query_groups, keys_new, preferred_element_type=jnp.float32
    )
    causal = (jnp.arange(step_count)[:, None] >= jnp.arange(step_count)[None, :])[
        None, :, None, None, :
    ]
    new_scores = jnp.where(causal, new_scores, NEGATIVE)
    attn_rows_dev = w_out.shape[0]
    top_max = lax.pmax(block_top, "seq")
    rescale = jnp.exp(block_top - top_max)
    total_sum, accumulated = lax.psum(
        (block_total * rescale, block_accum * rescale[..., None]), "seq"
    )
    highest = jnp.maximum(top_max, jnp.max(new_scores, axis=4))
    carried = jnp.exp(top_max - highest)
    new_probs = jnp.where(causal, jnp.exp(new_scores - highest[..., None]), 0.0)
    denominator = total_sum * carried + jnp.sum(new_probs, axis=4)
    numerator = accumulated * carried[..., None] + jnp.einsum(
        "rskgu,rukd->rskgd", new_probs, values_new.astype(jnp.float32)
    )
    attention = (
        (numerator / denominator[..., None])
        .astype(jnp.bfloat16)
        .reshape(rows_req, step_count, H * HD)
    )
    attention_cols = lax.dynamic_slice_in_dim(
        attention, seq_index * attn_rows_dev, attn_rows_dev, 2
    ).reshape(tokens, attn_rows_dev)
    out_part = jnp.dot(attention_cols, out_full, preferred_element_type=jnp.float32)
    attn_out = lax.psum(out_part, "seq")
    residual = hidden.reshape(tokens, D) + normalize(attn_out) * post_attn_gain
    ffn_in = (normalize(residual) * ffn_gain).astype(jnp.bfloat16)
    gate_out = jnp.dot(ffn_in, gate_full, preferred_element_type=jnp.float32)
    up_out = jnp.dot(ffn_in, up_full, preferred_element_type=jnp.float32)
    activated = (jax.nn.gelu(gate_out, approximate=True) * up_out).astype(jnp.bfloat16)
    down_part = jnp.dot(activated, down_full, preferred_element_type=jnp.float32)
    down_out = lax.psum(down_part, "seq")
    layer_out = residual + normalize(down_out) * post_ffn_gain
    return layer_out.astype(jnp.bfloat16).reshape(rows_req, step_count, D)


def solution(mesh):
    return jax.shard_map(
        on_device,
        mesh=mesh,
        in_specs=(
            P("req", None, None),
            P(),
            P(),
            P(),
            P(),
            P(),
            P(),
            P("seq", "req"),
            P("seq", "req"),
            P("req", "seq"),
            P("req", "seq"),
            P("seq", "req"),
            P("req", "seq", None),
            P("req", "seq", None),
            P("req", "seq", None),
            P("req", "seq", None),
            P("req"),
            P("req"),
            P("req"),
            P("req", None),
        ),
        out_specs=P("req", None, None),
        check_vma=False,
    )
```

profile of v0, /device:TPU:2, one launch (start us, length us, event | category | flops | bytes accessed | tf_op | source)
XLA Modules:
  0.0 1219.5 jit_solution(10066826392859031519)
XLA Ops:
  6.5 1.1 convert_element_type.35
  7.6 0.2 multiply_reduce_fusion.3
  7.8 0.7 copy-done.11
  8.6 15.6 %all_gather.15 = bf16[32,3072]{1,0:T(8,128)(2,1)S(1)} all-gather(bf16[32,384]{1,0:T(8,128)(2,1)S(1)} %copy-done.11), channel_id=1, replica_groups=mesh['seq'=64,'req'=8] {'req'}, dimensions={1}, use_global_device_ids=true | all-gather | bytes 221184 | tf_op jit(solution)/shard_map/all_gather | solution.py:54
  24.1 0.8 dynamic-slice
  24.9 0.1 fusion.48
  25.0 0.2 fusion.68
  25.2 0.2 reshape.248
  25.5 1.4 copy.120
  27.0 0.6 copy-done.15
  27.5 0.2 select_reduce_fusion
  27.8 13.0 %all_gather.16 = bf16[32,2048]{1,0:T(8,128)(2,1)S(1)} all-gather(bf16[32,256]{1,0:T(8,128)(2,1)S(1)} %copy-done.12), channel_id=1, replica_groups=mesh['seq'=64,'req'=8] {'req'}, dimensions={1}, use_global_device_ids=true | all-gather | bytes 147456 | tf_op jit(solution)/shard_map/all_gather | solution.py:55
  41.2 0.9 copy-done.4
  42.1 0.9 copy-done.5
  43.1 0.9 copy-done.6
  44.0 0.6 copy-done.20
  44.8 0.6 copy-done.19
  45.5 142.4 %all-reduce.5.cloned.1.call-done = f32[16,4,3072]{2,0,1:T(8,128)} async-done(((f32[16,4,3072]{2,0,1:T(8,128)}), f32[16,4,3072]{2,0,1:T(8,128)}) %all-reduce.5.cloned.1.call-update) | async-done | bytes 786448 | tf_op jit(solution)/shard_map/psum | solution.py:61
  187.8 1.1 slice_multiply_fusion
  189.0 0.2 copy.162
  189.2 0.1 reduce_sum.100
  189.4 0.4 reshape.249
  189.8 0.7 copy-done.16
  190.4 0.2 fusion.10
  190.6 0.4 fusion.65
  191.1 0.3 fusion.66
  191.4 277.1 %pmax.7 = f32[16,4,2,4]{0,3,1,2:T(4,128)S(1)} all-reduce(f32[16,4,2,4]{0,3,1,2:T(4,128)S(1)} %max.16), channel_id=1, replica_groups=mesh['seq'=64,'req'=8] {'seq'}, use_global_device_ids=true, to_apply=%region_6.7 | all-reduce | flops 512 | bytes 4096 | tf_op jit(solution)/shard_map/pmax | solution.py:133
  468.6 0.3 fusion.13
  468.8 0.3 fusion.11
  469.1 1.0 fusion.64
  470.2 0.1 multiply_reduce_fusion.5
  470.4 0.6 copy-done.17
  471.1 0.1 fusion.35
  471.2 1.3 fusion.67
  472.5 0.1 copy.131
  472.7 0.1 copy.132
  472.8 0.3 fusion.30
  473.1 0.1 copy.136
  473.2 273.9 %psum.37 = f32[16,4,2,4]{0,3,1,2:T(4,128)S(1)} all-reduce(f32[16,4,2,4]{0,3,1,2:T(4,128)S(1)} %bitcast.93), channel_id=1, replica_groups=mesh['seq'=64,'req'=8] {'seq'}, use_global_device_ids=true, to_apply=%region_13.14 | all-reduce | flops 512 | bytes 4096 | tf_op jit(solution)/shard_map/psum | solution.py:135
  747.2 0.3 convolution_bitcast_fusion
  747.4 1.1 fusion.3
  748.7 0.1 multiply_reduce_fusion.4
  748.9 0.1 fusion.36
  749.0 0.4 fusion.31
  749.5 149.1 %all-reduce.7.cloned.1.call-done = f32[16,4,2,4,256]{4,0,3,1,2:T(8,128)} async-done(((f32[16,4,2,4,256]{4,0,3,1,2:T(8,128)}), f32[16,4,2,4,256]{4,0,3,1,2:T(8,128)}) %all-reduce.7.cloned.1.call-update) | async-done | bytes 524304 | tf_op jit(solution)/shard_map/psum | solution.py:135
  898.6 1.4 fusion.8
  900.0 0.1 copy.137
  900.1 0.2 reshape.254
  900.4 1.0 fusion.69
  901.5 0.8 copy-done.7
  902.3 13.1 %all_gather.17 = bf16[2048,128]{1,0:T(8,128)(2,1)S(1)} all-gather(bf16[256,128]{1,0:T(8,128)(2,1)S(1)} %copy-done.7), channel_id=1, replica_groups=mesh['seq'=64,'req'=8] {'req'}, dimensions={0}, use_global_device_ids=true | all-gather | bytes 589824 | tf_op jit(solution)/shard_map/all_gather | solution.py:56
  915.4 0.8 copy-done.8
  916.2 13.2 %all_gather.18 = bf16[2048,128]{1,0:T(8,128)(2,1)S(1)} all-gather(bf16[256,128]{1,0:T(8,128)(2,1)S(1)} %copy-done.8), channel_id=1, replica_groups=mesh['seq'=64,'req'=8] {'req'}, dimensions={0}, use_global_device_ids=true | all-gather | bytes 589824 | tf_op jit(solution)/shard_map/all_gather | solution.py:57
  929.4 13.2 %all_gather.19 = bf16[128,2048]{1,0:T(8,128)(2,1)S(1)} all-gather(bf16[128,256]{1,0:T(8,128)(2,1)S(1)} %copy-done.9), channel_id=1, replica_groups=mesh['seq'=64,'req'=8] {'req'}, dimensions={1}, use_global_device_ids=true | all-gather | bytes 589824 | tf_op jit(solution)/shard_map/all_gather | solution.py:58
  942.6 111.9 %all-reduce.9.cloned.1.call-done = f32[64,2048]{1,0:T(8,128)} async-done(((f32[64,2048]{1,0:T(8,128)}), f32[64,2048]{1,0:T(8,128)}) %all-reduce.9.cloned.1.call-update) | async-done | bytes 524304 | tf_op jit(solution)/shard_map/psum | solution.py:154
  1054.6 1.2 multiply_reduce_fusion.2
  1055.9 0.3 multiply_reduce_fusion.1
  1056.1 0.4 copy-done.10
  1056.6 0.3 fusion.63
  1056.8 1.3 fusion.6
  1058.1 152.6 %all-reduce.11.cloned.1.call-done = f32[64,2048]{1,0:T(8,128)} async-done(((f32[64,2048]{1,0:T(8,128)}), f32[64,2048]{1,0:T(8,128)}) %all-reduce.11.cloned.1.call-update) | async-done | bytes 524304 | tf_op jit(solution)/shard_map/psum | solution.py:161
  1210.7 1.2 multiply_reduce_fusion
  1212.0 0.1 add_convert_fusion
  1212.1 0.8 reshape.256
  (70 shorter events, 1.6 us)
Async XLA Ops:
  6.5 181.3 %all-reduce.5.cloned.1.call-start = ((), (), s32[]{:S(2)}) async-start(), calls=%async_computation | async-start | bytes 1572864 | tf_op jit(solution)/shard_map/psum | solution.py:61
  6.5 1.1 copy-start
  7.8 0.7 copy-start.11
  26.8 0.7 copy-start.15
  26.8 0.9 copy-start.18
  26.8 14.2 %copy-start.3 = (bf16[1,256,512]{2,1,0:T(8,128)(2,1)S(1)}, bf16[1,256,512]{2,1,0:T(8,128)(2,1)}, u32[]{:S(2)}) copy-start(bf16[1,256,512]{2,1,0:T(8,128)(2,1)} %param.34) | copy-start | bytes 786436
  26.9 0.9 copy-start.12
  26.9 871.7 %all-reduce.7.cloned.1.call-start = ((), (), s32[]{:S(2)}) async-start(), calls=%async_computation.1 | async-start | bytes 1048576 | tf_op jit(solution)/shard_map/psum | solution.py:135
  41.1 1.0 copy-start.4
  42.0 1.0 copy-start.5
  43.0 0.9 copy-start.6
  44.0 0.7 copy-start.20
  44.7 0.7 copy-start.19
  189.7 0.7 copy-start.16
  470.4 0.7 copy-start.17
  748.6 306.0 %all-reduce.9.cloned.1.call-start = ((), (), s32[]{:S(2)}) async-start(), calls=%async_computation.2 | async-start | bytes 1048576 | tf_op jit(solution)/shard_map/psum | solution.py:154
  901.4 0.8 copy-start.7
  901.4 309.3 %all-reduce.11.cloned.1.call-start = ((), (), s32[]{:S(2)}) async-start(), calls=%async_computation.3 | async-start | bytes 1048576 | tf_op jit(solution)/shard_map/psum | solution.py:161
  915.4 0.8 copy-start.8
  916.2 13.2 %copy-start.9 = (bf16[128,256]{1,0:T(8,128)(2,1)S(1)}, bf16[128,256]{1,0:T(8,128)(2,1)}, u32[]{:S(2)}) copy-start(bf16[128,256]{1,0:T(8,128)(2,1)} %param.31) | copy-start | bytes 196612
  929.4 126.4 %copy-start.13 = (f32[2048]{0:T(1024)S(1)}, f32[2048]{0:T(1024)}, u32[]{:S(2)}) copy-start(f32[2048]{0:T(1024)} %param.24) | copy-start | bytes 24580
  1054.6 1.3 copy-start.2
  1055.9 0.7 copy-start.10
  1058.1 153.8 %copy-start.14 = (f32[2048]{0:T(1024)S(1)}, f32[2048]{0:T(1024)}, u32[]{:S(2)}) copy-start(f32[2048]{0:T(1024)} %param.26) | copy-start | bytes 24580
  1210.7 1.3 copy-start.1
Sparse Core Ops, SparseCore 0:
  27.0 160.8 all-reduce.4
  748.7 149.8 all-reduce.6
  902.1 152.4 all-reduce.8
  1058.3 152.3 all-reduce.10
where the time goes:
time: 1220 us
  blocking collectives  619 us (51%)
  waiting for transfers between devices  556 us (46%)
  local copies, waits for them, and re-layouts  14.7 us (1%)
  between operations  13.5 us (1%)
    pmax x1, blocking collectives, on_device(): top_max = lax.pmax(block_top, 'seq')  277 us
    psum x1, blocking collectives, on_device(): lax.psum((block_total * rescale, block_accum * rescale[..., None]), 'seq')  274 us
    psum x1, waiting for transfers between devices, on_device(): down_out = lax.psum(down_part, 'seq')  153 us
    psum x1, waiting for transfers between devices, on_device(): lax.psum((block_total * rescale, block_accum * rescale[..., None]), 'seq')  149 us
    psum x1, waiting for transfers between devices, on_device(): projected = lax.psum(qkv_part, 'seq').reshape(rows_req, step_count, QKV)  142 us
    psum x1, waiting for transfers between devices, on_device(): attn_out = lax.psum(out_part, 'seq')  112 us
  transfers between devices with their start and end apart: 4, of which 4 were waited for; matrix products, arithmetic and copies ran while one was open for 0% of the time, Pallas kernels for 0%

commit v1 on v0

--- a/solution.py
+++ b/solution.py
@@ -11,6 +11,7 @@
 QKV = 3072
 EPSILON = 1e-06
 NEGATIVE = -1e30
+unit_see = lambda array_in, peer_axis: jnp.sum(lax.all_gather(array_in, peer_axis), axis=0)
 
 
 def normalize(values):
@@ -58,7 +59,7 @@
         lax.all_gather(w_down, "req", axis=1, tiled=True),
     )
     qkv_part = jnp.dot(normed_cols, qkv_full, preferred_element_type=jnp.float32)
-    projected = lax.psum(qkv_part, "seq").reshape(rows_req, step_count, QKV)
+    projected = unit_see(qkv_part, "seq").reshape(rows_req, step_count, QKV)
     queries = (
         normalize(projected[..., : H * HD].reshape(rows_req, step_count, H, HD)) * q_gain
     ).astype(jnp.bfloat16)

time: 1220 us -> 1390 us (1.14)
  waiting for transfers between devices: 556 us -> 698 us
  other arithmetic: 9.17 us -> 36.4 us
    all_gather x0 -> x1, waiting for transfers between devices: none -> 283 us  [lax.all_gather(array_in, peer_axis)]
    psum x1 -> x0, waiting for transfers between devices: 142 us -> none  [on_device(): projected = lax.psum(qkv_part, 'seq').reshape(rows_req, step_count, QKV)]
    reduce_sum x0 -> x1, other arithmetic: none -> 17.2 us  [jnp.sum(lax.all_gather(array_in, peer_axis), axis=0)]
  transfers between devices with their start and end apart: 4 -> 4, of which waited for: 4 -> 4; matrix products, arithmetic and copies ran while one was open for 0% -> 1% of each run, Pallas kernels for 0% -> 0%
where the time goes in v1:
time: 1390 us
  waiting for transfers between devices  698 us (50%)
  blocking collectives  621 us (45%)
  other arithmetic  36.4 us (3%)
    all_gather x1, waiting for transfers between devices, lax.all_gather(array_in, peer_axis)  283 us
    pmax x1, blocking collectives, on_device(): top_max = lax.pmax(block_top, 'seq')  278 us
    psum x1, blocking collectives, on_device(): lax.psum((block_total * rescale, block_accum * rescale[..., None]), 'seq')  274 us
    psum x1, waiting for transfers between devices, on_device(): down_out = lax.psum(down_part, 'seq')  153 us
    psum x1, waiting for transfers between devices, on_device(): lax.psum((block_total * rescale, block_accum * rescale[..., None]), 'seq')  149 us
    psum x1, waiting for transfers between devices, on_device(): attn_out = lax.psum(out_part, 'seq')  113 us
  transfers between devices with their start and end apart: 4, of which 4 were waited for; matrix products, arithmetic and copies ran while one was open for 1% of the time, Pallas kernels for 0%

profile of v1, /device:TPU:2, one launch (start us, length us, event | category | flops | bytes accessed | tf_op | source)
XLA Modules:
  0.0 1389.7 jit_solution(4517494410401130023)
XLA Ops:
  6.5 1.1 convert_element_type.35
  7.6 1.2 multiply_reduce_fusion.3
  8.8 15.8 %all_gather.21 = bf16[32,3072]{1,0:T(8,128)(2,1)S(1)} all-gather(bf16[32,384]{1,0:T(8,128)(2,1)} %param.27), channel_id=1, replica_groups=mesh['seq'=64,'req'=8] {'req'}, dimensions={1}, use_global_device_ids=true | all-gather | bytes 221184 | tf_op jit(solution)/shard_map/all_gather | solution.py:55
  24.6 0.8 dynamic-slice
  25.3 0.1 fusion.48
  25.4 1.1 fusion.68
  26.7 0.9 select_reduce_fusion
  27.5 0.7 and_select_fusion.1
  28.5 1.0 reshape_squeeze.6
  29.5 1.0 reshape.250
  30.6 1.0 reshape.251
  31.6 1.0 reshape_squeeze.7
  32.6 13.2 all_gather.24
  45.8 0.6 iota_compare_fusion.1
  46.4 0.7 broadcast_compare_fusion
  47.2 0.7 broadcast_and_fusion
  47.8 1.3 fusion.53
  49.1 283.3 %all-gather.3.cloned.1.call-done = f32[4096,3072]{1,0:T(8,128)} async-done(((f32[64,3072]{1,0:T(8,128)}), f32[4096,3072]{1,0:T(8,128)}) %all-gather.3.cloned.1.call-update) | async-done | bytes 50331664 | tf_op jit(solution)/shard_map/all_gather | solution.py:14
  332.4 17.2 %reduce_sum.109 = f32[64,3072]{1,0:T(8,128)S(1)} reduce(f32[64,64,3072]{2,1,0:T(8,128)} %bitcast.61, f32[]{:T(128)} %constant.69.clone.1), dimensions={0}, to_apply=%region_1.0 | reduce | flops 12386304 | bytes 51118084 | tf_op jit(solution)/shard_map/reduce_sum | solution.py:14
  349.7 0.2 reshape.248
  349.9 0.2 slice_multiply_fusion
  350.2 0.3 mul.206
  350.4 0.2 reduce_sum.110
  350.7 0.4 reshape.266
  351.2 1.0 fusion.10
  352.2 1.2 fusion.65
  353.4 1.0 fusion.66
  354.4 277.7 %pmax.7 = f32[16,4,2,4]{0,3,1,2:T(4,128)S(1)} all-reduce(f32[16,4,2,4]{0,3,1,2:T(4,128)S(1)} %max.16), channel_id=1, replica_groups=mesh['seq'=64,'req'=8] {'seq'}, use_global_device_ids=true, to_apply=%region_6.7 | all-reduce | flops 512 | bytes 4096 | tf_op jit(solution)/shard_map/pmax | solution.py:134
  632.1 0.9 fusion.13
  633.1 1.0 fusion.11
  634.0 0.1 reshape.252
  634.2 0.2 multiply_reduce_fusion.5
  634.4 0.1 copy.129
  634.6 0.8 fusion.35
  635.4 2.0 fusion.67
  637.3 0.1 copy.132
  637.5 0.1 copy.135
  637.6 0.9 fusion.30
  638.6 0.1 copy.139
  638.7 273.9 %psum.29 = f32[16,4,2,4]{0,3,1,2:T(4,128)S(1)} all-reduce(f32[16,4,2,4]{0,3,1,2:T(4,128)S(1)} %bitcast.81), channel_id=1, replica_groups=mesh['seq'=64,'req'=8] {'seq'}, use_global_device_ids=true, to_apply=%region_13.14 | all-reduce | flops 512 | bytes 4096 | tf_op jit(solution)/shard_map/psum | solution.py:136
  912.7 1.0 convolution_bitcast_fusion
  913.6 1.8 fusion.3
  915.5 0.1 reshape.253
  915.6 0.2 multiply_reduce_fusion.4
  915.9 0.1 copy.134
  916.0 0.1 fusion.36
  916.1 1.1 fusion.31
  917.2 148.7 %all-reduce.4.cloned.1.call-done = f32[16,4,2,4,256]{4,0,3,1,2:T(8,128)} async-done(((f32[16,4,2,4,256]{4,0,3,1,2:T(8,128)}), f32[16,4,2,4,256]{4,0,3,1,2:T(8,128)}) %all-reduce.4.cloned.1.call-update) | async-done | bytes 524304 | tf_op jit(solution)/shard_map/psum | solution.py:136
  1065.9 1.4 fusion.8
  1067.3 0.1 copy.140
  1067.5 0.2 reshape.254
  1067.7 1.0 fusion.69
  1068.8 13.3 all_gather.25
  1082.2 13.3 all_gather.26
  1095.5 13.3 all_gather.27
  1108.8 113.1 %all-reduce.6.cloned.1.call-done = f32[64,2048]{1,0:T(8,128)} async-done(((f32[64,2048]{1,0:T(8,128)}), f32[64,2048]{1,0:T(8,128)}) %all-reduce.6.cloned.1.call-update) | async-done | bytes 524304 | tf_op jit(solution)/shard_map/psum | solution.py:155
  1221.9 1.2 multiply_reduce_fusion.2
  1223.1 1.3 multiply_reduce_fusion.1
  1224.5 1.0 fusion.63
  1225.4 2.0 fusion.6
  1227.4 152.6 %all-reduce.8.cloned.1.call-done = f32[64,2048]{1,0:T(8,128)} async-done(((f32[64,2048]{1,0:T(8,128)}), f32[64,2048]{1,0:T(8,128)}) %all-reduce.8.cloned.1.call-update) | async-done | bytes 524304 | tf_op jit(solution)/shard_map/psum | solution.py:162
  1380.0 1.2 multiply_reduce_fusion
  1381.2 1.2 add_convert_fusion
  1382.4 0.8 reshape.256
  (34 shorter events, 1.0 us)
Async XLA Ops:
  6.5 1075.6 %copy-start = (bf16[16,4,2048]{2,1,0:T(4,128)(2,1)S(1)}, bf16[16,4,2048]{2,1,0:T(4,128)(2,1)}, u32[]{:S(2)}) copy-start(bf16[16,4,2048]{2,1,0:T(4,128)(2,1)} %param.20) | copy-start | bytes 786436
  6.5 325.9 %all-gather.3.cloned.1.call-start = ((), (), s32[]{:S(2)}) async-start(), calls=%async_computation.3 | async-start | bytes 51118080 | tf_op jit(solution)/shard_map/all_gather | solution.py:14
  26.6 1039.3 %all-reduce.4.cloned.1.call-start = ((), (), s32[]{:S(2)}) async-start(), calls=%async_computation | async-start | bytes 1048576 | tf_op jit(solution)/shard_map/psum | solution.py:136
  915.4 306.5 %all-reduce.6.cloned.1.call-start = ((), (), s32[]{:S(2)}) async-start(), calls=%async_computation.1 | async-start | bytes 1048576 | tf_op jit(solution)/shard_map/psum | solution.py:155
  1068.8 311.2 %all-reduce.8.cloned.1.call-start = ((), (), s32[]{:S(2)}) async-start(), calls=%async_computation.2 | async-start | bytes 1048576 | tf_op jit(solution)/shard_map/psum | solution.py:162
Sparse Core Ops, SparseCore 0:
  26.7 305.6 all-gather.2
  915.5 150.3 all-reduce.3
  1069.5 152.4 all-reduce.5
  1227.6 152.3 all-reduce.7
